TPU v7x, 512 devices: a whole 4x8x8 slice. The times are simulated.
512 devices in a mesh: pipe: 32 (over z_hi, y), dp: 16 (over x, z_lo, core).
Axes of the slice: x: 4, y: 8, z: 8 (z_hi: 4, z_lo: 2; z = z_hi * 2 + z_lo), core: 2. Of those that a mesh axis runs over, the one named last changes fastest.
Arguments:
- section_inputs: bfloat16 [32, 3072, 6144], P('pipe', 'dp'), may hold values from -6 to 6
- loss_grad: bfloat16 [3072, 6144], P('dp', 'pipe'), may hold values from -6 to 6
- weight_blocks: bfloat16 [32, 48, 128, 128], P('pipe', 'dp'), may hold values from -0.3125 to 0.3125
- left_factor: bfloat16 [32, 6144, 64], P('pipe', 'dp'), may hold values from -0.078125 to 0.078125
- right_factor: bfloat16 [32, 64, 6144], P('pipe', None, 'dp'), may hold values from -0.5 to 0.5
- block_column: int32 [32, 48], P('pipe'), may hold values from 0 to 47, each once within a row
- live_length: int32 [16, 12], P('dp'), may hold values from 1 to 16, 144 in all within a row
Outputs:
- in_grad: bfloat16 [32, 3072, 6144], P('pipe', 'dp')
- grad_blocks: bfloat16 [32, 48, 128, 128], P('pipe', 'dp')
- grad_left: bfloat16 [32, 6144, 64], P('pipe', 'dp')
- grad_right: bfloat16 [32, 64, 6144], P('pipe', None, 'dp')
Inputs may be any that keep to these rules, and one draw needn't show every extreme that they name: `block_column`: each section's row is a permutation of 0 to 47. `live_length`: each row sums to 144 live tokens.
All inputs are finite; a program needn't handle non-finite values.
Results may differ from a plain program's by a relative error of at most 0.035.
Values may be sent and summed in bfloat16 or wider, within the bound.
A program may use at most 64 MiB of HBM per device.

v0:
```python
import math

import jax
import jax.numpy as jnp
from jax import lax
from jax.sharding import PartitionSpec as P


def shifted(shard, axis, by):
    count = lax.axis_size(axis)
    pairs = [(i, i + by) for i in range(count) if 0 <= i + by < count]
    return lax.ppermute(shard, axis, pairs)


def slope_of(values):
    cumulative = 0.5 * (1.0 + jax.scipy.special.erf(values * (1.0 / math.sqrt(2.0))))
    density = jnp.exp(-0.5 * values * values) * (1.0 / math.sqrt(2.0 * math.pi))
    return cumulative + values * density


def inverse_of(columns):
    number = columns.shape[0]
    ladder = jnp.arange(number, dtype=jnp.int32)
    matches = (columns[:, None] == ladder[None, :]).astype(jnp.int32)
    return jnp.sum(matches * ladder[:, None], axis=0)


def section_rows(inputs, incoming, blocks, left_whole, right_whole, columns, inverse):
    row_count, features = inputs.shape
    number, block_size = (blocks.shape[0], blocks.shape[1])
    split_in = inputs.reshape(row_count, number, block_size)
    sparse = jnp.einsum("tnb,nbc->tnc", split_in, blocks, preferred_element_type=jnp.float32)
    sparse = jnp.take(sparse, inverse, axis=1).reshape(row_count, features)
    lowered = jnp.dot(inputs, left_whole, preferred_element_type=jnp.float32).astype(jnp.bfloat16)
    preactivation = sparse + jnp.dot(lowered, right_whole, preferred_element_type=jnp.float32)
    delta_grad = (incoming.astype(jnp.float32) * slope_of(preactivation)).astype(jnp.bfloat16)
    delta_split = jnp.take(delta_grad.reshape(row_count, number, block_size), columns, axis=1)
    back_sparse = jnp.einsum(
        "tnc,nbc->tnb", delta_split, blocks, preferred_element_type=jnp.float32
    ).reshape(row_count, features)
    reduced = jnp.einsum(
        "td,rd->tr", delta_grad, right_whole, preferred_element_type=jnp.float32
    ).astype(jnp.bfloat16)
    back_low = jnp.einsum("tr,dr->td", reduced, left_whole, preferred_element_type=jnp.float32)
    outgoing = (incoming.astype(jnp.float32) + back_sparse + back_low).astype(jnp.bfloat16)
    return (outgoing, delta_split, lowered, reduced)


def weight_terms(inputs, delta_split, lowered, reduced):
    row_count, features = inputs.shape
    number, block_size = (delta_split.shape[1], delta_split.shape[2])
    split_in = inputs.reshape(row_count, number, block_size)
    grad_blocks = jnp.einsum(
        "tnb,tnc->nbc", split_in, delta_split, preferred_element_type=jnp.float32
    )
    grad_left = jnp.einsum("td,tr->dr", inputs, reduced, preferred_element_type=jnp.float32)
    grad_mixed = jnp.einsum("tr,tnc->rnc", lowered, delta_split, preferred_element_type=jnp.float32)
    return (grad_blocks, grad_left, grad_mixed)


def replace_rows(buffer, fresh, start, active):
    older = lax.dynamic_slice_in_dim(buffer, start, fresh.shape[0], 0)
    return lax.dynamic_update_slice_in_dim(buffer, jnp.where(active, fresh, older), start, 0)


def body(
    section_inputs, loss_grad, weight_blocks, left_factor, right_factor, block_column, live_length
):
    inputs = section_inputs[0]
    blocks, left_whole, right_whole = (
        lax.all_gather(weight_blocks[0], "dp", axis=0, tiled=True),
        lax.all_gather(left_factor[0], "dp", axis=0, tiled=True),
        lax.all_gather(right_factor[0], "dp", axis=1, tiled=True),
    )
    head = lax.all_gather(loss_grad, "pipe", axis=1, tiled=True)
    columns = block_column[0]
    inverse = inverse_of(columns)
    sections = lax.axis_size("pipe")
    section = lax.axis_index("pipe")
    token_count, features = inputs.shape
    micro_count = live_length.shape[1]
    micro_rows = token_count // micro_count
    number, block_size = (blocks.shape[0], blocks.shape[1])
    rank_width = left_whole.shape[1]
    positions = jnp.arange(token_count, dtype=jnp.int32)
    owners = (positions // micro_rows)[:, None] == jnp.arange(micro_count, dtype=jnp.int32)[None, :]
    limits = jnp.sum(jnp.where(owners, live_length[0][None, :], 0), axis=1)
    live_rows = positions % micro_rows < limits
    seeded = jnp.where(live_rows[:, None], head, jnp.zeros_like(head))
    work_count = inputs.shape[0]
    turns = micro_count + sections - 1
    stored = (
        jnp.zeros((work_count, number, block_size), jnp.bfloat16),
        jnp.zeros((work_count, rank_width), jnp.bfloat16),
        jnp.zeros((work_count, rank_width), jnp.bfloat16),
    )

    def compute(upstream, rows_in):
        return section_rows(rows_in, upstream, blocks, left_whole, right_whole, columns, inverse)

    def skipped(upstream, rows_in):
        return (
            jnp.zeros_like(upstream),
            jnp.zeros((micro_rows, number, block_size), jnp.bfloat16),
            jnp.zeros((micro_rows, rank_width), jnp.bfloat16),
            jnp.zeros((micro_rows, rank_width), jnp.bfloat16),
        )

    def turn(index, carry):
        incoming, grads_out, saved = carry
        micro = index - (sections - 1 - section)
        active = (micro >= 0) & (micro < micro_count)
        start = jnp.clip(micro, 0, micro_count - 1) * micro_rows
        rows_in = lax.dynamic_slice_in_dim(inputs, start, micro_rows, 0)
        from_head = lax.dynamic_slice_in_dim(seeded, start, micro_rows, 0)
        upstream = jnp.where(section == sections - 1, from_head, incoming)
        outgoing, delta_split, lowered, reduced = lax.cond(
            active, compute, skipped, upstream, rows_in
        )
        grads_out = replace_rows(grads_out, outgoing, start, active)
        saved = (
            replace_rows(saved[0], delta_split, start, active),
            replace_rows(saved[1], lowered, start, active),
            replace_rows(saved[2], reduced, start, active),
        )
        passed = shifted(outgoing, "pipe", -1)
        return (passed, grads_out, saved)

    start_grad = jnp.zeros((micro_rows, features), jnp.bfloat16)
    unused, work_grad, saved = lax.fori_loop(
        0, turns, turn, (start_grad, jnp.zeros_like(inputs), stored)
    )
    grad_blocks, grad_left, grad_mixed = weight_terms(inputs, saved[0], saved[1], saved[2])
    grad_right = jnp.take(grad_mixed, inverse, axis=1).reshape(rank_width, features)
    sum_blocks, sum_left, sum_right = (
        lax.psum_scatter(
            grad_blocks.astype(jnp.bfloat16), "dp", scatter_dimension=0, tiled=True
        ).astype(jnp.float32),
        lax.psum_scatter(
            grad_left.astype(jnp.bfloat16), "dp", scatter_dimension=0, tiled=True
        ).astype(jnp.float32),
        lax.psum_scatter(
            grad_right.astype(jnp.bfloat16), "dp", scatter_dimension=1, tiled=True
        ).astype(jnp.float32),
    )
    return (
        work_grad[None],
        sum_blocks.astype(jnp.bfloat16)[None],
        sum_left.astype(jnp.bfloat16)[None],
        sum_right.astype(jnp.bfloat16)[None],
    )


def solution(mesh):
    in_specs = (
        P("pipe", "dp", None),
        P("dp", "pipe"),
        P("pipe", "dp", None, None),
        P("pipe", "dp", None),
        P("pipe", None, "dp"),
        P("pipe", None),
        P("dp", None),
    )
    out_specs = (
        P("pipe", "dp", None),
        P("pipe", "dp", None, None),
        P("pipe", "dp", None),
        P("pipe", None, "dp"),
    )
    return jax.shard_map(body, mesh=mesh, in_specs=in_specs, out_specs=out_specs, check_vma=False)
```

profile of v0, /device:TPU:1, one launch (start us, length us, event | category | flops | bytes accessed | tf_op | source)
XLA Modules:
  0.0 1397.8 jit_solution(17293354459489336557)
XLA Ops:
  15.0 34.3 %all-gather.1 = bf16[1,6144,64]{2,1,0:T(8,128)(2,1)S(1)} all-gather(bf16[1,384,64]{2,1,0:T(8,128)(2,1)S(1)} %copy.44), channel_id=3, replica_groups=mesh['pipe'=32,'dp'=16] {'dp'}, dimensions={1}, use_global_device_ids=true | all-gather | bytes 835584 | tf_op jit(solution)/shard_map/all_gather | solution.py:72
  49.3 21.6 %all-gather.2 = bf16[1,64,6144]{2,1,0:T(8,128)(2,1)} all-gather(bf16[1,64,384]{2,1,0:T(8,128)(2,1)} %param.15), channel_id=4, replica_groups=mesh['pipe'=32,'dp'=16] {'dp'}, dimensions={2}, use_global_device_ids=true | all-gather | bytes 835584 | tf_op jit(solution)/shard_map/all_gather | solution.py:73
  70.9 38.8 %all-gather.6.cloned.1.call-done = bf16[192,6144]{0,1:T(8,128)(2,1)} async-done(((bf16[192,192]{0,1:T(8,128)(2,1)}), bf16[192,6144]{0,1:T(8,128)(2,1)}) %all-gather.6.cloned.1.call-update) | async-done | bytes 2359312 | tf_op jit(solution)/shard_map/all_gather | solution.py:75
  118.0 30.0 %all-gather.8.cloned.1.call-done = bf16[1,48,128,128]{3,2,0,1:T(8,128)(2,1)} async-done(((bf16[1,3,128,128]{3,2,0,1:T(8,128)(2,1)}), bf16[1,48,128,128]{3,2,0,1:T(8,128)(2,1)}) %all-gather.8.cloned.1.call-update) | async-done | bytes 1572880 | tf_op jit(solution)/shard_map/all_gather | solution.py:71
  153.6 995.3 %while.23 = (s32[]{:T(128)}, bf16[16,6144]{1,0:T(8,128)(2,1)}, bf16[192,6144]{1,0:T(8,128)(2,1)}, bf16[192,48,128]{2,0,1:T(8,128)(2,1)}, bf16[192,64]{1,0:T(8,12...) while((s32[]{:T(128)}, bf16[16,6144]{1,0:T(8,128)(2,1)}, ...), condition=%wide.region_5.6_spmd, body=%wide.region_2.5_spmd.sunk | while | flops 102833008 | bytes 20126928 | solution.py:130
  265.0 6.9 collective-permute-done
  321.8 5.5 collective-permute-done
  451.6 8.7 collective-permute-done
  469.0 5.5 collective-permute-done
  535.7 288.8 %collective-permute-done = bf16[16,6144]{1,0:T(8,128)(2,1)S(1)} collective-permute-done((bf16[16,6144]{1,0:T(8,128)(2,1)}, bf16[16,6144]{1,0:T(8,128)(2,1)S(1)}, u32[]{:S(2)}, u32[]{:S(2)}) %collective-permute-start) | collective-permute-done | bytes 196640 | tf_op jit(solution)/shard_map/while/body/eval_jaxpr/ppermute | solution.py:12
  825.3 14.4 %conditional.2 = (bf16[16,6144]{1,0:T(8,128)(2,1)}, bf16[16,48,128]{2,0,1:T(8,128)(2,1)}, bf16[16,64]{1,0:T(8,128)(2,1)S(1)}, bf16[16,64]{1,0:T(8,128)(2,1)}) conditional(s32[]{:T(128)} %convert_element_type.80, () %tuple.65, (pred[]{:T(512)}, bf16[192,6144]{1,0:T(8,128)(2,1)}, s32[]{:T(128)}, bf16[16,6144]{1,0:T(8,128)(2,1)}, s32[48]{0:T(128)}, ...), branch_computations={%region_3.3_spmd, %region_4.4_spmd} | conditional | flops 102634336 | bytes 17349906 | solution.py:117
  845.9 5.7 collective-permute-done
  852.3 14.4 %conditional.2 = (bf16[16,6144]{1,0:T(8,128)(2,1)}, bf16[16,48,128]{2,0,1:T(8,128)(2,1)}, bf16[16,64]{1,0:T(8,128)(2,1)S(1)}, bf16[16,64]{1,0:T(8,128)(2,1)}) conditional(s32[]{:T(128)} %convert_element_type.80, () %tuple.65, (pred[]{:T(512)}, bf16[192,6144]{1,0:T(8,128)(2,1)}, s32[]{:T(128)}, bf16[16,6144]{1,0:T(8,128)(2,1)}, s32[48]{0:T(128)}, ...), branch_computations={%region_3.3_spmd, %region_4.4_spmd} | conditional | flops 102634336 | bytes 17349906 | solution.py:117
  879.0 14.4 %conditional.2 = (bf16[16,6144]{1,0:T(8,128)(2,1)}, bf16[16,48,128]{2,0,1:T(8,128)(2,1)}, bf16[16,64]{1,0:T(8,128)(2,1)S(1)}, bf16[16,64]{1,0:T(8,128)(2,1)}) conditional(s32[]{:T(128)} %convert_element_type.80, () %tuple.65, (pred[]{:T(512)}, bf16[192,6144]{1,0:T(8,128)(2,1)}, s32[]{:T(128)}, bf16[16,6144]{1,0:T(8,128)(2,1)}, s32[48]{0:T(128)}, ...), branch_computations={%region_3.3_spmd, %region_4.4_spmd} | conditional | flops 102634336 | bytes 17349906 | solution.py:117
  899.6 6.9 collective-permute-done
  907.3 14.4 %conditional.2 = (bf16[16,6144]{1,0:T(8,128)(2,1)}, bf16[16,48,128]{2,0,1:T(8,128)(2,1)}, bf16[16,64]{1,0:T(8,128)(2,1)S(1)}, bf16[16,64]{1,0:T(8,128)(2,1)}) conditional(s32[]{:T(128)} %convert_element_type.80, () %tuple.65, (pred[]{:T(512)}, bf16[192,6144]{1,0:T(8,128)(2,1)}, s32[]{:T(128)}, bf16[16,6144]{1,0:T(8,128)(2,1)}, s32[48]{0:T(128)}, ...), branch_computations={%region_3.3_spmd, %region_4.4_spmd} | conditional | flops 102634336 | bytes 17349906 | solution.py:117
  927.8 8.5 collective-permute-done
  937.1 14.4 %conditional.2 = (bf16[16,6144]{1,0:T(8,128)(2,1)}, bf16[16,48,128]{2,0,1:T(8,128)(2,1)}, bf16[16,64]{1,0:T(8,128)(2,1)S(1)}, bf16[16,64]{1,0:T(8,128)(2,1)}) conditional(s32[]{:T(128)} %convert_element_type.80, () %tuple.65, (pred[]{:T(512)}, bf16[192,6144]{1,0:T(8,128)(2,1)}, s32[]{:T(128)}, bf16[16,6144]{1,0:T(8,128)(2,1)}, s32[48]{0:T(128)}, ...), branch_computations={%region_3.3_spmd, %region_4.4_spmd} | conditional | flops 102634336 | bytes 17349906 | solution.py:117
  957.6 7.5 collective-permute-done
  965.9 14.4 %conditional.2 = (bf16[16,6144]{1,0:T(8,128)(2,1)}, bf16[16,48,128]{2,0,1:T(8,128)(2,1)}, bf16[16,64]{1,0:T(8,128)(2,1)S(1)}, bf16[16,64]{1,0:T(8,128)(2,1)}) conditional(s32[]{:T(128)} %convert_element_type.80, () %tuple.65, (pred[]{:T(512)}, bf16[192,6144]{1,0:T(8,128)(2,1)}, s32[]{:T(128)}, bf16[16,6144]{1,0:T(8,128)(2,1)}, s32[48]{0:T(128)}, ...), branch_computations={%region_3.3_spmd, %region_4.4_spmd} | conditional | flops 102634336 | bytes 17349906 | solution.py:117
  986.4 7.0 collective-permute-done
  994.2 14.4 %conditional.2 = (bf16[16,6144]{1,0:T(8,128)(2,1)}, bf16[16,48,128]{2,0,1:T(8,128)(2,1)}, bf16[16,64]{1,0:T(8,128)(2,1)S(1)}, bf16[16,64]{1,0:T(8,128)(2,1)}) conditional(s32[]{:T(128)} %convert_element_type.80, () %tuple.65, (pred[]{:T(512)}, bf16[192,6144]{1,0:T(8,128)(2,1)}, s32[]{:T(128)}, bf16[16,6144]{1,0:T(8,128)(2,1)}, s32[48]{0:T(128)}, ...), branch_computations={%region_3.3_spmd, %region_4.4_spmd} | conditional | flops 102634336 | bytes 17349906 | solution.py:117
  1020.6 14.4 %conditional.2 = (bf16[16,6144]{1,0:T(8,128)(2,1)}, bf16[16,48,128]{2,0,1:T(8,128)(2,1)}, bf16[16,64]{1,0:T(8,128)(2,1)S(1)}, bf16[16,64]{1,0:T(8,128)(2,1)}) conditional(s32[]{:T(128)} %convert_element_type.80, () %tuple.65, (pred[]{:T(512)}, bf16[192,6144]{1,0:T(8,128)(2,1)}, s32[]{:T(128)}, bf16[16,6144]{1,0:T(8,128)(2,1)}, s32[48]{0:T(128)}, ...), branch_computations={%region_3.3_spmd, %region_4.4_spmd} | conditional | flops 102634336 | bytes 17349906 | solution.py:117
  1041.2 6.1 collective-permute-done
  1048.0 14.4 %conditional.2 = (bf16[16,6144]{1,0:T(8,128)(2,1)}, bf16[16,48,128]{2,0,1:T(8,128)(2,1)}, bf16[16,64]{1,0:T(8,128)(2,1)S(1)}, bf16[16,64]{1,0:T(8,128)(2,1)}) conditional(s32[]{:T(128)} %convert_element_type.80, () %tuple.65, (pred[]{:T(512)}, bf16[192,6144]{1,0:T(8,128)(2,1)}, s32[]{:T(128)}, bf16[16,6144]{1,0:T(8,128)(2,1)}, s32[48]{0:T(128)}, ...), branch_computations={%region_3.3_spmd, %region_4.4_spmd} | conditional | flops 102634336 | bytes 17349906 | solution.py:117
  1068.5 5.9 collective-permute-done
  1075.2 14.4 %conditional.2 = (bf16[16,6144]{1,0:T(8,128)(2,1)}, bf16[16,48,128]{2,0,1:T(8,128)(2,1)}, bf16[16,64]{1,0:T(8,128)(2,1)S(1)}, bf16[16,64]{1,0:T(8,128)(2,1)}) conditional(s32[]{:T(128)} %convert_element_type.80, () %tuple.65, (pred[]{:T(512)}, bf16[192,6144]{1,0:T(8,128)(2,1)}, s32[]{:T(128)}, bf16[16,6144]{1,0:T(8,128)(2,1)}, s32[48]{0:T(128)}, ...), branch_computations={%region_3.3_spmd, %region_4.4_spmd} | conditional | flops 102634336 | bytes 17349906 | solution.py:117
  1101.3 14.4 %conditional.2 = (bf16[16,6144]{1,0:T(8,128)(2,1)}, bf16[16,48,128]{2,0,1:T(8,128)(2,1)}, bf16[16,64]{1,0:T(8,128)(2,1)S(1)}, bf16[16,64]{1,0:T(8,128)(2,1)}) conditional(s32[]{:T(128)} %convert_element_type.80, () %tuple.65, (pred[]{:T(512)}, bf16[192,6144]{1,0:T(8,128)(2,1)}, s32[]{:T(128)}, bf16[16,6144]{1,0:T(8,128)(2,1)}, s32[48]{0:T(128)}, ...), branch_computations={%region_3.3_spmd, %region_4.4_spmd} | conditional | flops 102634336 | bytes 17349906 | solution.py:117
  1127.3 14.3 %conditional.2 = (bf16[16,6144]{1,0:T(8,128)(2,1)}, bf16[16,48,128]{2,0,1:T(8,128)(2,1)}, bf16[16,64]{1,0:T(8,128)(2,1)S(1)}, bf16[16,64]{1,0:T(8,128)(2,1)}) conditional(s32[]{:T(128)} %convert_element_type.80, () %tuple.65, (pred[]{:T(512)}, bf16[192,6144]{1,0:T(8,128)(2,1)}, s32[]{:T(128)}, bf16[16,6144]{1,0:T(8,128)(2,1)}, s32[48]{0:T(128)}, ...), branch_computations={%region_3.3_spmd, %region_4.4_spmd} | conditional | flops 102634336 | bytes 17349906 | solution.py:117
  1162.4 87.8 %reduce-scatter.12.cloned.1.call-done = bf16[384,64]{1,0:T(8,128)(2,1)} async-done(((bf16[6144,64]{1,0:T(8,128)(2,1)}), bf16[384,64]{1,0:T(8,128)(2,1)}) %reduce-scatter.12.cloned.1.call-update) | async-done | bytes 49168
  1251.8 68.1 %reduce-scatter.10.cloned.1.call-done = bf16[384,64]{1,0:T(8,128)(2,1)} async-done(((bf16[6144,64]{1,0:T(8,128)(2,1)}), bf16[384,64]{1,0:T(8,128)(2,1)}) %reduce-scatter.10.cloned.1.call-update) | async-done | bytes 49168
  1321.5 68.1 %reduce-scatter.8.cloned.1.call-done = bf16[3,128,128]{1,2,0:T(8,128)(2,1)} async-done(((bf16[48,128,128]{1,2,0:T(8,128)(2,1)}), bf16[3,128,128]{1,2,0:T(8,128)(2,1)}) %reduce-scatter.8.cloned.1.call-update) | async-done | bytes 98320 | tf_op jit(solution)/shard_map/reduce_scatter | solution.py:136
  (814 shorter events, 732.9 us)
Async XLA Ops:
  7.2 102.5 %all-gather.6.cloned.1.call-start = ((), (), s32[]{:S(2)}) async-start(), calls=%async_computation.3 | async-start | bytes 3244032 | tf_op jit(solution)/shard_map/all_gather | solution.py:75
  8.9 139.1 %all-gather.8.cloned.1.call-start = ((), (), s32[]{:S(2)}) async-start(), calls=%async_computation.5 | async-start | bytes 1671168 | tf_op jit(solution)/shard_map/all_gather | solution.py:71
  9.6 1240.6 %reduce-scatter.12.cloned.1.call-start = ((), (), s32[]{:S(2)}) async-start(), calls=%async_computation.7 | async-start | bytes 1671168
  259.0 12.9 collective-permute-start
  274.6 11.2 collective-permute-start
  288.5 10.6 collective-permute-start
  301.8 11.4 collective-permute-start
  315.9 11.4 collective-permute-start
  342.5 10.4 collective-permute-start
  355.6 10.8 collective-permute-start
  405.1 11.4 collective-permute-start
  419.2 11.2 collective-permute-start
  433.0 9.9 collective-permute-start
  445.6 14.6 %collective-permute-start = (bf16[16,6144]{1,0:T(8,128)(2,1)}, bf16[16,6144]{1,0:T(8,128)(2,1)S(1)}, u32[]{:S(2)}, u32[]{:S(2)}) collective-permute-start(bf16[16,6144]{1,0:T(8,128)(2,1)} %get-tuple-element.597), channel_id=1, source_target_pairs={{16,0},{32,16},{48,32},{64,48},{80,64},{96,80},{112,96},{128,112},... | collective-permute-start | bytes 589832 | tf_op jit(solution)/shard_map/while/body/eval_jaxpr/ppermute | solution.py:12
  463.0 11.5 collective-permute-start
  477.2 11.3 collective-permute-start
  491.2 10.2 collective-permute-start
  504.1 11.3 collective-permute-start
  529.8 294.8 %collective-permute-start = (bf16[16,6144]{1,0:T(8,128)(2,1)}, bf16[16,6144]{1,0:T(8,128)(2,1)S(1)}, u32[]{:S(2)}, u32[]{:S(2)}) collective-permute-start(bf16[16,6144]{1,0:T(8,128)(2,1)} %get-tuple-element.597), channel_id=1, source_target_pairs={{16,0},{32,16},{48,32},{64,48},{80,64},{96,80},{112,96},{128,112},... | collective-permute-start | bytes 589832 | tf_op jit(solution)/shard_map/while/body/eval_jaxpr/ppermute | solution.py:12
  839.7 11.9 collective-permute-start
  866.7 11.6 collective-permute-start
  893.5 13.1 collective-permute-start
  921.7 14.7 %collective-permute-start = (bf16[16,6144]{1,0:T(8,128)(2,1)}, bf16[16,6144]{1,0:T(8,128)(2,1)S(1)}, u32[]{:S(2)}, u32[]{:S(2)}) collective-permute-start(bf16[16,6144]{1,0:T(8,128)(2,1)} %get-tuple-element.597), channel_id=1, source_target_pairs={{16,0},{32,16},{48,32},{64,48},{80,64},{96,80},{112,96},{128,112},... | collective-permute-start | bytes 589832 | tf_op jit(solution)/shard_map/while/body/eval_jaxpr/ppermute | solution.py:12
  951.5 13.7 collective-permute-start
  980.3 13.2 collective-permute-start
  1008.6 11.3 collective-permute-start
  1035.0 12.2 collective-permute-start
  1062.4 12.1 collective-permute-start
  1089.6 11.0 collective-permute-start
  1115.8 10.8 collective-permute-start
  1153.8 166.2 %reduce-scatter.10.cloned.1.call-start = ((), (), s32[]{:S(2)}) async-start(), calls=%async_computation.6 | async-start | bytes 1671168
  1157.7 232.0 %reduce-scatter.8.cloned.1.call-start = ((), (), s32[]{:S(2)}) async-start(), calls=%async_computation.4 | async-start | bytes 1671168 | tf_op jit(solution)/shard_map/reduce_scatter | solution.py:136
  (135 other events, 392.0 us)
Sparse Core Ops, SparseCore 0:
  11.7 97.8 all-gather.5
  111.8 36.1 all-gather.7
  1153.9 96.2 reduce-scatter.11
  1252.9 67.0 reduce-scatter.9
  1322.6 66.9 reduce-scatter.7
where the time goes:
time: 1410 us; the launch traced here: 1400 us
  waiting for transfers between devices  765 us (54%)
  other arithmetic  237 us (17%)
  local copies, waits for them, and re-layouts  150 us (11%)
  matrix products  120 us (9%)
  blocking collectives  55.9 us (4%)
  starting transfers between devices  55.2 us (4%)
    ppermute x43, waiting for transfers between devices, shifted(): return lax.ppermute(shard, axis, pairs)  471 us
    dynamic_update_slice x129, other arithmetic, replace_rows(): lax.dynamic_update_slice_in_dim(buffer, jnp.where(active, fresh, older),...  203 us
    unnamed x7, waiting for transfers between devices  157 us
    reduce_scatter x1, waiting for transfers between devices, body(): lax.psum_scatter(grad_blocks.astype(jnp.bfloat16), 'dp', scatter_dimensio...  68.1 us
    another operation x128, local copies, waits for them, and re-layouts  65.9 us
    ppermute x43, starting transfers between devices, shifted(): return lax.ppermute(shard, axis, pairs)  55 us
    all_gather x1, waiting for transfers between devices, body(): head = lax.all_gather(loss_grad, 'pipe', axis=1, tiled=True)  38.8 us
    all_gather x1, blocking collectives, body(): lax.all_gather(left_factor[0], 'dp', axis=0, tiled=True)  34.3 us
  transfers between devices with their start and end apart: 48, of which 48 were waited for; matrix products, arithmetic and copies ran while one was open for 16% of the time, Pallas kernels for 0%

commit v1 on v0

v1 whole, which is shorter than its diff:
```python
import functools
import math

import jax
import jax.numpy as jnp
from jax import lax
from jax.experimental import pallas as pl
from jax.experimental.pallas import tpu as pltpu
from jax.sharding import PartitionSpec as P

MESH = pl.DeviceIdType.MESH
LIVE = 144
ROWS = 16
CHUNKS = 4
VMEM = pl.BlockSpec(memory_space=pltpu.VMEM)
SMEM = pl.BlockSpec(memory_space=pltpu.SMEM)
LIMIT = 60 * 1024 * 1024


def slope_of(values):
    cumulative = 0.5 * (1.0 + jax.scipy.special.erf(values * (1.0 / math.sqrt(2.0))))
    density = jnp.exp(-0.5 * values * values) * (1.0 / math.sqrt(2.0 * math.pi))
    return cumulative + values * density


def inverse_of(columns):
    number = columns.shape[0]
    ladder = jnp.arange(number, dtype=jnp.int32)
    matches = (columns[:, None] == ladder[None, :]).astype(jnp.int32)
    return jnp.sum(matches * ladder[:, None], axis=0)


def greet_group(count, me):
    barrier = pltpu.get_barrier_semaphore()
    for by in range(1, count):
        pl.semaphore_signal(
            barrier, inc=1, device_id={"dp": lax.rem(me + by, count)}, device_id_type=MESH
        )
    pl.semaphore_wait(barrier, count - 1)


def gather_kernel(count, own_ref, whole_ref, send_sem, recv_sem, local_sem):
    me = lax.axis_index("dp")
    greet_group(count, me)
    copies = []
    for by in range(1, count):
        copy = pltpu.make_async_remote_copy(
            src_ref=own_ref,
            dst_ref=whole_ref.at[me],
            send_sem=send_sem.at[by],
            recv_sem=recv_sem.at[by],
            device_id={"dp": lax.rem(me + by, count)},
            device_id_type=MESH,
        )
        copy.start()
        copies.append(copy)
    local = pltpu.make_async_copy(own_ref, whole_ref.at[me], local_sem)
    local.start()
    local.wait()
    for copy in copies:
        copy.wait()


def gather_dp(own, count):
    return pl.pallas_call(
        functools.partial(gather_kernel, count),
        out_shape=jax.ShapeDtypeStruct((count,) + own.shape, own.dtype),
        in_specs=[VMEM],
        out_specs=VMEM,
        scratch_shapes=[
            pltpu.SemaphoreType.DMA((count,)),
            pltpu.SemaphoreType.DMA((count,)),
            pltpu.SemaphoreType.DMA,
        ],
        compiler_params=pltpu.CompilerParams(
            collective_id=0, has_side_effects=True, vmem_limit_bytes=LIMIT
        ),
    )(own)


def reduce_kernel(count, parts_ref, sum_ref, landed, send_sem, recv_sem, local_sem):
    me = lax.axis_index("dp")
    greet_group(count, me)
    copies = []
    for by in range(1, count):
        target = lax.rem(me + by, count)
        copy = pltpu.make_async_remote_copy(
            src_ref=parts_ref.at[target],
            dst_ref=landed.at[by],
            send_sem=send_sem.at[by],
            recv_sem=recv_sem.at[by],
            device_id={"dp": target},
            device_id_type=MESH,
        )
        copy.start()
        copies.append(copy)
    local = pltpu.make_async_copy(parts_ref.at[me], landed.at[0], local_sem)
    local.start()
    local.wait()
    for copy in copies:
        copy.wait()
    height = 64

    def some_rows(at, carry):
        rows = pl.ds(at * height, height)
        total = jnp.sum(landed[:, rows, :].astype(jnp.float32), axis=0)
        sum_ref[rows, :] = total.astype(sum_ref.dtype)
        return carry

    lax.fori_loop(0, sum_ref.shape[0] // height, some_rows, 0)


def reduce_dp(parts):
    count = parts.shape[0]
    return pl.pallas_call(
        functools.partial(reduce_kernel, count),
        out_shape=jax.ShapeDtypeStruct(parts.shape[1:], parts.dtype),
        in_specs=[VMEM],
        out_specs=VMEM,
        scratch_shapes=[
            pltpu.VMEM(parts.shape, parts.dtype),
            pltpu.SemaphoreType.DMA((count,)),
            pltpu.SemaphoreType.DMA((count,)),
            pltpu.SemaphoreType.DMA,
        ],
        compiler_params=pltpu.CompilerParams(
            collective_id=1, has_side_effects=True, vmem_limit_bytes=LIMIT
        ),
    )(parts)


def pipe_kernel(
    sections,
    cols_ref,
    head_ref,
    slope_ref,
    mats_ref,
    left_ref,
    out_ref,
    delta_ref,
    red_ref,
    g_ref,
    back_ref,
    send_sem,
    recv_sem,
):
    section = lax.axis_index("pipe")
    last = sections - 1
    after = lax.rem(section + sections - 1, sections)
    steps, number, rows, width = g_ref.shape
    rank = left_ref.shape[0]
    span = number // CHUNKS
    barrier = pltpu.get_barrier_semaphore()

    for neighbour in (after, lax.rem(section + 1, sections)):
        pl.semaphore_signal(barrier, inc=1, device_id={"pipe": neighbour}, device_id_type=MESH)
    pl.semaphore_wait(barrier, 2)

    def hop(step, chunk):
        part = pl.ds(chunk * span, span)
        return pltpu.make_async_remote_copy(
            src_ref=out_ref.at[step, part],
            dst_ref=g_ref.at[step, part],
            send_sem=send_sem.at[step * CHUNKS + chunk],
            recv_sem=recv_sem.at[step * CHUNKS + chunk],
            device_id={"pipe": after},
            device_id_type=MESH,
        )

    def one_step(step, carry):
        here = pl.ds(pl.multiple_of(step * rows, rows), rows)
        total = jnp.zeros((rows, rank), jnp.float32)
        for chunk in range(CHUNKS):
            part = pl.ds(chunk * span, span)

            @pl.when(section == last)
            def _():
                g_ref[step, part] = head_ref[step, part]

            @pl.when(section < last)
            def _():
                hop(step, chunk).wait_recv()

            delta = g_ref[step, part].astype(jnp.float32) * slope_ref[part, here, :]
            delta = delta.astype(jnp.bfloat16)
            delta_ref[part, here, :] = delta
            both = lax.dot_general(
                delta,
                mats_ref[part],
                (((2,), (1,)), ((0,), (0,))),
                preferred_element_type=jnp.float32,
            )
            back_ref[part] = both[:, :, :width]
            total = total + jnp.sum(both[:, :, width:], axis=0)
        reduced = total.astype(jnp.bfloat16)
        red_ref[here, :] = reduced
        for chunk in range(CHUNKS):
            low = jnp.dot(
                reduced,
                left_ref[:, chunk * span * width : (chunk + 1) * span * width],
                preferred_element_type=jnp.float32,
            )
            for at in range(span):
                block = chunk * span + at
                fresh = g_ref[step, block].astype(jnp.float32) + back_ref[cols_ref[block]]
                fresh = fresh + low[:, at * width : (at + 1) * width]
                out_ref[step, block] = fresh.astype(jnp.bfloat16)

            @pl.when(section > 0)
            def _():
                hop(step, chunk).start()

        return carry

    lax.fori_loop(0, steps, one_step, 0)

    @pl.when(section > 0)
    def _():
        def drain(step, carry):
            for chunk in range(CHUNKS):
                hop(step, chunk).wait_send()
            return carry

        lax.fori_loop(0, steps, drain, 0)


def run_pipe(sections, columns, head, slope, mats, left_turned):
    steps, number, rows, width = head.shape
    rank = left_turned.shape[0]
    return pl.pallas_call(
        functools.partial(pipe_kernel, sections),
        out_shape=(
            jax.ShapeDtypeStruct(head.shape, jnp.bfloat16),
            jax.ShapeDtypeStruct((number, steps * rows, width), jnp.bfloat16),
            jax.ShapeDtypeStruct((steps * rows, rank), jnp.bfloat16),
        ),
        in_specs=[SMEM, VMEM, VMEM, VMEM, VMEM],
        out_specs=(VMEM, VMEM, VMEM),
        scratch_shapes=[
            pltpu.VMEM(head.shape, jnp.bfloat16),
            pltpu.VMEM((number, rows, width), jnp.float32),
            pltpu.SemaphoreType.DMA((steps * CHUNKS,)),
            pltpu.SemaphoreType.DMA((steps * CHUNKS,)),
        ],
        compiler_params=pltpu.CompilerParams(
            collective_id=2, has_side_effects=True, vmem_limit_bytes=LIMIT
        ),
    )(columns, head, slope, mats, left_turned)


def body(
    section_inputs, loss_grad, weight_blocks, left_factor, right_factor, block_column, live_length
):
    inputs = section_inputs[0]
    columns = block_column[0]
    inverse = inverse_of(columns)
    sections = lax.axis_size("pipe")
    group = lax.axis_size("dp")
    tokens, features = inputs.shape
    micro_count = live_length.shape[1]
    micro_rows = tokens // micro_count
    own_blocks, width = weight_blocks.shape[1], weight_blocks.shape[2]
    number = own_blocks * group
    rank = left_factor.shape[2]
    steps = LIVE // ROWS

    own = jnp.concatenate(
        [
            weight_blocks[0].reshape(own_blocks * width, width),
            jnp.concatenate([left_factor[0], right_factor[0].T], axis=1),
        ],
        axis=0,
    )
    whole = gather_dp(own, group)
    blocks = whole[:, : own_blocks * width].reshape(number, width, width)
    left = whole[:, own_blocks * width :, :rank].reshape(features, rank)
    right_turned = whole[:, own_blocks * width :, rank:].reshape(number, width, rank)
    blocks_at = jnp.take(blocks, inverse, axis=0)
    mats = jnp.concatenate([jnp.swapaxes(blocks_at, 1, 2), right_turned], axis=2)

    lengths = live_length[0]
    micro = jnp.arange(micro_count, dtype=jnp.int32)
    starts = jnp.sum(jnp.where(micro[None, :] < micro[:, None], lengths[None, :], 0), axis=1)
    inside = jnp.arange(micro_rows, dtype=jnp.int32)
    place = jnp.where(inside[None, :] < lengths[:, None], starts[:, None] + inside[None, :], LIVE)
    place = place.reshape(tokens)
    chosen = (jnp.arange(LIVE, dtype=jnp.int32)[:, None] == place[None, :]).astype(jnp.bfloat16)

    seeds = jnp.dot(chosen, loss_grad, preferred_element_type=jnp.float32).astype(jnp.bfloat16)
    head = lax.all_gather(seeds, "pipe", axis=1, tiled=True)
    head = jnp.swapaxes(head.reshape(steps, ROWS, number, width), 1, 2)

    live = jnp.dot(chosen, inputs, preferred_element_type=jnp.float32).astype(jnp.bfloat16)
    live_blocks = jnp.swapaxes(live.reshape(LIVE, number, width), 0, 1)
    live_at = jnp.take(live_blocks, inverse, axis=0)
    lowered = jnp.dot(live, left, preferred_element_type=jnp.float32).astype(jnp.bfloat16)
    before = jnp.einsum("jtb,jbc->jtc", live_at, blocks_at, preferred_element_type=jnp.float32)
    before = before + jnp.einsum(
        "tr,jcr->jtc", lowered, right_turned, preferred_element_type=jnp.float32
    )
    slope = slope_of(before)

    outgoing, delta, reduced = run_pipe(sections, columns, head, slope, mats, left.T)

    flat = jnp.swapaxes(outgoing, 1, 2).reshape(LIVE, features)
    in_grad = lax.dot_general(
        chosen, flat, (((0,), (0,)), ((), ())), preferred_element_type=jnp.float32
    ).astype(jnp.bfloat16)

    grad_at = jnp.einsum("jtb,jtc->jbc", live_at, delta, preferred_element_type=jnp.float32)
    grad_blocks = jnp.take(grad_at.astype(jnp.bfloat16), columns, axis=0)
    grad_left = jnp.einsum("td,tr->dr", live, reduced, preferred_element_type=jnp.float32)
    grad_right = jnp.einsum("jtc,tr->jcr", delta, lowered, preferred_element_type=jnp.float32)
    factors = jnp.concatenate([grad_left, grad_right.reshape(features, rank)], axis=1)
    parts = jnp.concatenate(
        [
            grad_blocks.reshape(group, own_blocks * width, width),
            factors.astype(jnp.bfloat16).reshape(group, features // group, 2 * rank),
        ],
        axis=1,
    )
    sums = reduce_dp(parts)
    sum_factors = sums[own_blocks * width :]
    return (
        in_grad[None],
        sums[: own_blocks * width].reshape(1, own_blocks, width, width),
        sum_factors[None, :, :rank],
        sum_factors[:, rank:].T[None],
    )


def solution(mesh):
    in_specs = (
        P("pipe", "dp", None),
        P("dp", "pipe"),
        P("pipe", "dp", None, None),
        P("pipe", "dp", None),
        P("pipe", None, "dp"),
        P("pipe", None),
        P("dp", None),
    )
    out_specs = (
        P("pipe", "dp", None),
        P("pipe", "dp", None, None),
        P("pipe", "dp", None),
        P("pipe", None, "dp"),
    )
    return jax.shard_map(body, mesh=mesh, in_specs=in_specs, out_specs=out_specs, check_vma=False)
```

time: 1410 us -> 450 us (0.32)
  waiting for transfers between devices: 765 us -> 8.36 us
  Pallas kernels: 0 us -> 349 us
  other arithmetic: 237 us -> 13.2 us
  matrix products: 120 us -> 15.2 us
  local copies, waits for them, and re-layouts: 150 us -> 49.2 us
  blocking collectives: 55.9 us -> 0 us
  starting transfers between devices: 55.2 us -> 0.04 us
    ppermute x43 -> x0, waiting for transfers between devices: 471 us -> none  [shifted(): return lax.ppermute(shard, axis, pairs)]
    pallas_call x0 -> x3, Pallas kernels: none -> 349 us  [the longest x1 232 us: run_pipe(): pl.pallas_call(functools.partial(pipe_kernel, sections), out_shape=(jax.S...]
    dynamic_update_slice x129 -> x0, other arithmetic: 203 us -> none  [replace_rows(): lax.dynamic_update_slice_in_dim(buffer, jnp.where(active, fresh, older),...]
    unnamed x7 -> x1, waiting for transfers between devices: 157 us -> 0.02 us
    dot_general x75 -> x9, matrix products: 120 us -> 15.2 us  [the longest x1 3.95 us: body(): jnp.einsum('jtb,jtc->jbc', live_at, delta, preferred_element_type=jnp.flo...]
    reduce_scatter x1 -> x0, waiting for transfers between devices: 68.1 us -> none  [body(): lax.psum_scatter(grad_blocks.astype(jnp.bfloat16), 'dp', scatter_dimensio...]
    another operation x128 -> x2, local copies, waits for them, and re-layouts: 65.9 us -> 4 us
    all_gather x2 -> x1, waiting for transfers between devices: 68.8 us -> 8.34 us  [body(): head = lax.all_gather(seeds, 'pipe', axis=1, tiled=True)]
  transfers between devices with their start and end apart: 48 -> 1, of which waited for: 48 -> 1; matrix products, arithmetic and copies ran while one was open for 16% -> 7% of each run, Pallas kernels for 0% -> 11%
where the time goes in v1:
time: 450 us
  Pallas kernels  349 us (78%)
  local copies, waits for them, and re-layouts  49.2 us (11%)
  matrix products  15.2 us (3%)
  between operations  14.3 us (3%)
  other arithmetic  13.2 us (3%)
  waiting for transfers between devices  8.36 us (2%)
    pallas_call x1, Pallas kernels, run_pipe(): pl.pallas_call(functools.partial(pipe_kernel, sections), out_shape=(jax.S...  232 us
    pallas_call x1, Pallas kernels, reduce_dp(): pl.pallas_call(functools.partial(reduce_kernel, count), out_shape=jax.Sha...  68 us
    pallas_call x1, Pallas kernels, gather_dp(): pl.pallas_call(functools.partial(gather_kernel, count), out_shape=jax.Sha...  49.3 us
    unnamed x54, local copies, waits for them, and re-layouts  13.7 us
  transfers between devices with their start and end apart: 1, of which 1 were waited for; matrix products, arithmetic and copies ran while one was open for 7% of the time, Pallas kernels for 11%

profile of v1, /device:TPU:1, one launch (start us, length us, event | category | flops | bytes accessed | tf_op | source)
XLA Modules:
  0.0 449.6 jit_solution(8721279574713791146)
XLA Ops:
  9.0 1.7 fusion.8
  12.5 1.7 maximum_maximum_fusion.1.own_ref
  14.2 49.3 %shard_map.102 = bf16[16,768,128]{2,1,0:T(8,128)(2,1)} custom-call(bf16[768,128]{1,0:T(8,128)(2,1)} %maximum_maximum_fusion.1.own_ref), custom_call_target="tpu_custom_call" | custom-call | tf_op jit(solution)/shard_map/pallas_call | solution.py:65
  63.5 2.9 slice.21
  66.4 2.3 fusion.18
  68.8 3.4 gather_fusion.1
  72.2 2.6 copy.53
  74.8 2.4 copy.64
  77.9 1.2 copy-done.1
  79.1 1.5 bitcast_bitcast_fusion
  80.6 3.6 gather_fusion
  84.8 1.6 fusion.11
  86.4 2.6 pad_maximum_fusion.mats_ref
  91.0 1.2 fusion.10
  92.1 3.1 fusion.4.slope_ref
  95.2 8.3 %all-gather.3.cloned.1.call-done = bf16[32,192,144]{1,2,0:T(8,128)(2,1)} async-done(((bf16[1,192,144]{1,2,0:T(8,128)(2,1)}), bf16[32,192,144]{1,2,0:T(8,128)(2,1)}) %all-gather.3.cloned.1.call-update) | async-done | bytes 1769488 | tf_op jit(solution)/shard_map/all_gather | solution.py:290
  103.6 3.9 copy.48
  107.5 4.8 %reshape.131 = bf16[6144,144]{0,1:T(8,128)(2,1)} reshape(bf16[32,192,144]{1,0,2:T(8,128)(2,1)} %copy.48) | data formatting | bytes 3538944
  112.3 1.8 copy.66
  114.1 1.7 copy.74
  115.8 232.0 %shard_map.103 = (bf16[9,48,16,128]{3,2,1,0:T(8,128)(2,1)}, bf16[48,144,128]{2,1,0:T(8,128)(2,1)}, bf16[144,64]{1,0:T(8,128)(2,1)}) custom-call(s32[48]{0:T(128)} %bitcast.95, bf16[9,48,16,128]{3,2,1,0:T(8,128)(2,1)} %bitcast.79, f32[48,144,128]{2,1,0:T(8,128)} %fusion.4.slope_ref, bf16[48,128,192]{2,1,0:T(8,128)(2,1)} %pad_maximum_fusion.mats_ref, ...), custom_call_target="tpu_custom_call" | custom-call | tf_op jit(solution)/shard_map/pallas_call | solution.py:230
  347.8 3.9 convolution_convert_fusion.3
  353.3 1.3 convolution_convert_fusion.2
  354.6 1.5 copy.59
  356.1 2.5 copy.58
  358.6 3.5 gather_fusion.2
  362.1 1.8 broadcast_select_fusion.1
  364.5 2.7 maximum_maximum_fusion.parts_ref
  367.2 68.0 %shard_map.104 = bf16[768,128]{1,0:T(8,128)(2,1)} custom-call(bf16[16,768,128]{2,1,0:T(8,128)(2,1)} %maximum_maximum_fusion.parts_ref), custom_call_target="tpu_custom_call" | custom-call | tf_op jit(solution)/shard_map/pallas_call | solution.py:115
  435.2 1.5 slice.24
  436.7 1.7 slice_bitcast_fusion
  439.1 2.2 fusion
  (69 shorter events, 11.1 us)
Async XLA Ops:
  7.2 70.1 %copy-start = (bf16[1,192,6144]{2,1,0:T(8,128)(2,1)S(1)}, bf16[1,192,6144]{2,1,0:T(8,128)(2,1)}, u32[]{:S(2)}) copy-start(bf16[1,192,6144]{2,1,0:T(8,128)(2,1)} %param.9) | copy-start | bytes 7077892
  7.2 96.4 %all-gather.3.cloned.1.call-start = ((), (), s32[]{:S(2)}) async-start(), calls=%async_computation | async-start | bytes 2433024 | tf_op jit(solution)/shard_map/all_gather | solution.py:290
  9.0 68.3 %copy-start.19 = (s32[192]{0:T(256)}, s32[192]{0:T(256)S(1)}, u32[]{:S(2)}) copy-start(s32[192]{0:T(256)S(1)} %select_n.43) | copy-start | bytes 2308
  63.5 2.9 copy-start.4
  66.4 2.3 copy-start.22
  77.9 1.2 copy-start.1
  84.2 2.2 copy-start.9
  84.8 5.5 %copy-start.21 = (pred[48]{0:T(512)(128)(4,1)}, pred[48]{0:T(512)(128)(4,1)S(1)}, u32[]{:S(2)}) copy-start(pred[48]{0:T(512)(128)(4,1)S(1)} %compare_and_fusion.1) | copy-start | bytes 148
  86.4 3.1 copy-start.2
  86.4 3.1 copy-start.5
  89.0 1.4 copy-start.6
  89.0 2.0 copy-start.7
  91.0 1.2 copy-start.16
  115.8 232.0 %copy-start.8 = (bf16[48,144,128]{2,1,0:T(8,128)(2,1)S(1)}, bf16[48,144,128]{2,1,0:T(8,128)(2,1)}, u32[]{:S(2)}) copy-start(bf16[48,144,128]{2,1,0:T(8,128)(2,1)} %gather_fusion) | copy-start | bytes 5308420
  347.8 4.0 copy-start.13
  347.8 4.0 copy-start.17
  351.8 1.5 copy-start.3
  351.8 1.5 copy-start.18
  358.6 3.5 copy-start.23
  362.1 1.9 copy-start.10
  362.1 2.4 copy-start.11
  367.2 71.3 %copy-start.12 = (bf16[9,48,16,128]{3,2,1,0:T(8,128)(2,1)S(1)}, bf16[9,48,16,128]{3,2,1,0:T(8,128)(2,1)}, u32[]{:S(2)}) copy-start(bf16[9,48,16,128]{3,2,1,0:T(8,128)(2,1)} %get-tuple-element.8) | copy-start | bytes 5308420
  438.4 0.6 copy-start.20
  439.0 2.2 copy-start.15
  439.0 3.0 copy-start.14
Sparse Core Ops, SparseCore 0:
  11.7 91.8 all-gather.2
